TPU v7x, 32 devices: a whole 2x2x4 slice. The times are simulated.
32 devices in a mesh: wide: 8 (over z, y), fields: 4 (over x, core).
Axes of the slice: x: 2, y: 2, z: 4, core: 2. Of those that a mesh axis runs over, the one named last changes fastest.
Arguments:
- vectors: float32 [256, 16384], P('wide', 'fields'), may hold values from 0.03 to 82, as said below
- pivot_ids: int32 [8], replicated, may hold values from 0 to 255
Outputs:
- similarity: float32 [256, 4, 256], P('wide', None, 'fields')
Inputs may be any that keep to these rules, and one draw needn't show every extreme that they name: `vectors`: every entry is positive.
All inputs are finite; a program needn't handle non-finite values.
Results may differ from a plain program's by a relative error of at most 0.0003.
Values sent between devices are 32-bit elements; how exact they have to be, the bound alone decides.
A program may use at most 64 MiB of HBM per device.

v0:
```python
import jax
import jax.numpy as jnp
from jax import lax
from jax.sharding import PartitionSpec as P

STEPS = 4


def from_behind(value, axis, steps):
    count = lax.axis_size(axis)
    pairs = [(source, (source + steps) % count) for source in range(count)]
    return lax.ppermute(value, axis, pairs)


def triple_table(owned, pivots, minima, partner):
    with_pivot = jnp.sum(minima, axis=-1)
    pivot_side = jnp.sum(jnp.minimum(pivots[:, None, :], partner[None, :, :]), axis=-1)
    pair_side = jnp.sum(jnp.minimum(owned[:, None, :], partner[None, :, :]), axis=-1)
    triple = lax.map(
        lambda layer: jnp.sum(jnp.minimum(layer[:, None, :], partner[None, :, :]), axis=-1),
        jnp.transpose(minima, (1, 0, 2)),
    )
    return (
        with_pivot[:, :, None]
        + pivot_side[None, :, :]
        + pair_side[:, None, :]
        - jnp.transpose(triple, (1, 0, 2))
    )


def body(vectors, pivot_ids):
    row_count = vectors.shape[0]
    pivot_count = pivot_ids.shape[0]
    first_row = lax.axis_index("wide") * row_count
    chosen = (
        pivot_ids[:, None] == first_row + jnp.arange(row_count, dtype=jnp.int32)[None, :]
    ).astype(jnp.float32)
    pivot_part = jnp.dot(
        chosen, vectors, precision=lax.Precision.HIGHEST, preferred_element_type=jnp.float32
    )
    pivots = lax.psum(pivot_part, "wide")
    owned_total, pivot_total = lax.psum(
        (jnp.sum(vectors, axis=1), jnp.sum(pivots, axis=1)), "fields"
    )
    minima = jnp.minimum(vectors[:, None, :], pivots[None, :, :])
    partner, partner_total = (vectors, owned_total)
    numerators = []
    partner_totals = []
    for stride in range(1, STEPS + 1):
        partner, partner_total = from_behind((partner, partner_total), "wide", 1)
        partner_totals.append(partner_total)
        numerator = triple_table(vectors, pivots, minima, partner).reshape(
            row_count, pivot_count * row_count
        )
        numerators.append(numerator)
    stacked = jnp.stack(numerators, axis=1)
    shares = lax.psum_scatter(stacked, "fields", scatter_dimension=2, tiled=True)
    share_width = shares.shape[2]
    offset = lax.axis_index("fields") * share_width
    step_totals = jnp.stack(partner_totals, axis=0)
    denominator = (
        owned_total[:, None, None, None]
        + pivot_total[None, None, :, None]
        + step_totals[None, :, None, :]
    )
    denominator = denominator.reshape(row_count, STEPS, pivot_count * row_count)
    denominator = lax.dynamic_slice_in_dim(denominator, offset, share_width, 2)
    return 1.5 * shares / denominator


def solution(mesh):
    placed = (P("wide", "fields"), P())
    return jax.shard_map(
        body, mesh=mesh, in_specs=placed, out_specs=P("wide", None, "fields"), check_vma=False
    )
```

profile of v0, /device:TPU:0, one launch (start us, length us, event | category | flops | bytes accessed | tf_op | source)
XLA Modules:
  0.0 292.2 jit_solution(9529471152527923765)
XLA Ops:
  6.5 3.0 %collective-permute-start = (f32[32,4096]{1,0:T(8,128)}, f32[32,4096]{1,0:T(8,128)S(1)}, u32[]{:S(2)}, u32[]{:S(2)}) collective-permute-start(f32[32,4096]{1,0:T(8,128)} %param.10), channel_id=1, source_target_pairs={{0,4},{4,8},{8,12},{12,16},{16,20},{20,24},{24,28},{28,0},{1,5},{5... | collective-permute-start | bytes 1572872 | tf_op jit(solution)/shard_map/ppermute | solution.py:12
  9.5 15.2 %collective-permute-done = f32[32,4096]{1,0:T(8,128)S(1)} collective-permute-done((f32[32,4096]{1,0:T(8,128)}, f32[32,4096]{1,0:T(8,128)S(1)}, u32[]{:S(2)}, u32[]{:S(2)}) %collective-permute-start) | collective-permute-done | bytes 524320 | tf_op jit(solution)/shard_map/ppermute | solution.py:12
  24.7 15.8 %collective-permute-done.1 = f32[32,4096]{1,0:T(8,128)S(1)} collective-permute-done((f32[32,4096]{1,0:T(8,128)S(1)}, f32[32,4096]{1,0:T(8,128)S(1)}, u32[]{:S(2)}, u32[]{:S(2)}) %collective-permute-start.1) | collective-permute-done | bytes 524320 | tf_op jit(solution)/shard_map/ppermute | solution.py:12
  40.5 2.0 fusion
  42.6 13.3 %collective-permute-done.2 = f32[32,4096]{1,0:T(8,128)S(1)} collective-permute-done((f32[32,4096]{1,0:T(8,128)S(1)}, f32[32,4096]{1,0:T(8,128)S(1)}, u32[]{:S(2)}, u32[]{:S(2)}) %collective-permute-start.2) | collective-permute-done | bytes 524320 | tf_op jit(solution)/shard_map/ppermute | solution.py:12
  55.8 1.2 reduce_sum.156
  57.0 65.4 %all-reduce.3.cloned.1.call-done = f32[8,4096]{1,0:T(8,128)} async-done(((f32[8,4096]{1,0:T(8,128)}), f32[8,4096]{1,0:T(8,128)}) %all-reduce.3.cloned.1.call-update) | async-done | bytes 131088 | tf_op jit(solution)/shard_map/psum | solution.py:41
  123.4 5.7 %all-reduce = (f32[32]{0:T(128)S(1)}, f32[8]{0:T(128)S(1)}) all-reduce(f32[32]{0:T(128)S(1)} %reduce_sum.156, f32[8]{0:T(128)S(1)} %reduce_sum.157), channel_id=1, replica_groups=mesh['wide'=8,'fields'=4] {'fields'}, use_global_device_ids=true, to_apply=%region_24.25 | all-reduce | flops 40 | bytes 320 | tf_op jit(solution)/shard_map/psum | solution.py:42
  129.8 5.6 %collective-permute-done.4 = f32[32]{0:T(128)S(1)} collective-permute-done((f32[32]{0:T(128)S(1)}, f32[32]{0:T(128)S(1)}, u32[]{:S(2)}, u32[]{:S(2)}) %collective-permute-start.4) | collective-permute-done | bytes 160 | tf_op jit(solution)/shard_map/ppermute | solution.py:12
  135.4 1.5 minimum_reduce_fusion.12
  137.0 4.7 %collective-permute-done.5 = f32[32]{0:T(128)S(1)} collective-permute-done((f32[32]{0:T(128)S(1)}, f32[32]{0:T(128)S(1)}, u32[]{:S(2)}, u32[]{:S(2)}) %collective-permute-start.5) | collective-permute-done | bytes 160 | tf_op jit(solution)/shard_map/ppermute | solution.py:12
  141.9 6.1 %collective-permute-done.6 = f32[32]{0:T(128)S(1)} collective-permute-done((f32[32]{0:T(128)S(1)}, f32[32]{0:T(128)S(1)}, u32[]{:S(2)}, u32[]{:S(2)}) %collective-permute-start.6) | collective-permute-done | bytes 160 | tf_op jit(solution)/shard_map/ppermute | solution.py:12
  147.9 5.3 %minimum_reduce_fusion.11 = (f32[8,32]{1,0:T(8,128)S(1)}, f32[8,32]{1,0:T(8,128)S(1)}, f32[8,32]{1,0:T(8,128)S(1)}, f32[8,32]{1,0:T(8,128)S(1)}, f32[8,32,4096]{2,1,0:T(8,128)}) fusion(f32[32,4096]{1,0:T(8,128)S(1)} %collective-permute-done, f32[8,4096]{1,0:T(8,128)} %all-reduce.3.cloned.1.call-done, f32[32,4096]{1,0:T(8,128)S(1)} %collective-permute-done.1, ...), kind=kLoop, calls=%fused_computation.19 | loop fusion | flops 9436160 | bytes 6950912 | tf_op jit(solution)/shard_map/reduce_sum | solution.py:17
  153.2 25.6 %while.40 = (s32[]{:T(128)}, f32[8,32,32]{2,1,0:T(8,128)S(1)}, f32[8,32,4096]{2,1,0:T(8,128)}, f32[32,4096]{1,0:T(8,128)S(1)}, s32[]{:T(128)}) while((s32[]{:T(128)}, f32[8,32,32]{2,1,0:T(8,128)S(1)}, f32[8,32,4096]{2,1,0:T(8,128)}, f32[32,4096]{1,0:T(8,128)S(1)}, s32[]{:T(128)}) %tuple.67), condition=%wide.region_6.0_spmd, body=%wide.region_4.6_spmd.sunk | while | flops 8387586 | bytes 2134093 | solution.py:19
  153.4 1.1 dynamic-slice_bitcast_fusion.8
  154.5 2.1 minimum_reduce_fusion.17
  156.6 1.1 dynamic-slice_bitcast_fusion.8
  157.7 2.1 minimum_reduce_fusion.17
  159.8 1.1 dynamic-slice_bitcast_fusion.8
  160.8 2.1 minimum_reduce_fusion.17
  162.9 1.1 dynamic-slice_bitcast_fusion.8
  164.0 2.1 minimum_reduce_fusion.17
  166.1 1.1 dynamic-slice_bitcast_fusion.8
  167.2 2.1 minimum_reduce_fusion.17
  169.3 1.1 dynamic-slice_bitcast_fusion.8
  170.4 2.1 minimum_reduce_fusion.17
  173.6 2.1 minimum_reduce_fusion.17
  176.7 2.1 minimum_reduce_fusion.17
  178.9 25.4 %while.41 = (s32[]{:T(128)}, f32[8,32,32]{2,1,0:T(8,128)S(1)}, f32[8,32,4096]{2,1,0:T(8,128)}, f32[32,4096]{1,0:T(8,128)S(1)}, s32[]{:T(128)}) while((s32[]{:T(128)}, f32[8,32,32]{2,1,0:T(8,128)S(1)}, f32[8,32,4096]{2,1,0:T(8,128)}, f32[32,4096]{1,0:T(8,128)S(1)}, s32[]{:T(128)}) %tuple.83), condition=%wide.region_11.12_spmd, body=%wide.region_9.11_spmd.sunk | while | flops 8387586 | bytes 2134093 | solution.py:19
  179.9 2.1 minimum_reduce_fusion.18
  182.0 1.1 dynamic-slice_bitcast_fusion.9
  183.1 2.1 minimum_reduce_fusion.18
  186.3 2.1 minimum_reduce_fusion.18
  189.5 2.1 minimum_reduce_fusion.18
  191.6 1.1 dynamic-slice_bitcast_fusion.9
  192.7 2.1 minimum_reduce_fusion.18
  195.8 2.1 minimum_reduce_fusion.18
  199.0 2.1 minimum_reduce_fusion.18
  202.2 2.1 minimum_reduce_fusion.18
  204.3 25.4 %while.42 = (s32[]{:T(128)}, f32[8,32,32]{2,1,0:T(8,128)S(1)}, f32[8,32,4096]{2,1,0:T(8,128)}, f32[32,4096]{1,0:T(8,128)S(1)}, s32[]{:T(128)}) while((s32[]{:T(128)}, f32[8,32,32]{2,1,0:T(8,128)S(1)}, f32[8,32,4096]{2,1,0:T(8,128)}, f32[32,4096]{1,0:T(8,128)S(1)}, s32[]{:T(128)}) %tuple.84), condition=%wide.region_16.17_spmd, body=%wide.region_14.16_spmd.sunk | while | flops 8387586 | bytes 2134093 | solution.py:19
  204.3 1.1 dynamic-slice_bitcast_fusion.10
  205.4 2.1 minimum_reduce_fusion.19
  208.6 2.1 minimum_reduce_fusion.19
  211.8 2.1 minimum_reduce_fusion.19
  213.9 1.1 dynamic-slice_bitcast_fusion.10
  214.9 2.1 minimum_reduce_fusion.19
  218.1 2.1 minimum_reduce_fusion.19
  221.3 2.1 minimum_reduce_fusion.19
  224.5 2.1 minimum_reduce_fusion.19
  227.7 2.1 minimum_reduce_fusion.19
  229.8 25.5 %while.43 = (s32[]{:T(128)}, f32[8,32,32]{2,1,0:T(8,128)S(1)}, f32[8,32,4096]{2,1,0:T(8,128)}, f32[32,4096]{1,0:T(8,128)S(1)}, s32[]{:T(128)}) while((s32[]{:T(128)}, f32[8,32,32]{2,1,0:T(8,128)S(1)}, f32[8,32,4096]{2,1,0:T(8,128)}, f32[32,4096]{1,0:T(8,128)S(1)}, s32[]{:T(128)}) %tuple.85), condition=%wide.region_21.22_spmd, body=%wide.region_19.21_spmd.sunk | while | flops 8387586 | bytes 2134093 | solution.py:19
  229.8 1.1 dynamic-slice_bitcast_fusion.11
  230.9 2.1 minimum_reduce_fusion.20
  234.1 2.1 minimum_reduce_fusion.20
  237.3 2.1 minimum_reduce_fusion.20
  239.4 1.1 dynamic-slice_bitcast_fusion.11
  240.5 2.1 minimum_reduce_fusion.20
  243.6 2.1 minimum_reduce_fusion.20
  246.8 2.1 minimum_reduce_fusion.20
  248.9 1.1 dynamic-slice_bitcast_fusion.11
  250.0 2.1 minimum_reduce_fusion.20
  253.2 2.1 minimum_reduce_fusion.20
  255.3 4.9 %minimum_reduce_fusion.7 = (f32[32,32]{1,0:T(8,128)S(1)}, f32[32,32]{1,0:T(8,128)S(1)}, f32[32,32]{1,0:T(8,128)S(1)}, f32[32,32]{1,0:T(8,128)S(1)}) fusion(f32[32,4096]{1,0:T(8,128)S(1)} %get-tuple-element.311, f32[32,4096]{1,0:T(8,128)S(1)} %copy-done, f32[32,4096]{1,0:T(8,128)S(1)} %get-tuple-element.314, f32[32,4096]{1,0:T(8,128)S(1)} %get-tuple-element.317, ...), kind=kLoop, calls=%fused_computation.15 | loop fusion | flops 33550336 | bytes 2637824 | tf_op jit(solution)/shard_map/reduce_sum | solution.py:18
  262.6 21.2 %reduce-scatter.4.cloned.1.call-done = f32[64,128]{1,0:T(8,128)} async-done(((f32[256,128]{1,0:T(8,128)}), f32[64,128]{1,0:T(8,128)}) %reduce-scatter.4.cloned.1.call-update) | async-done | bytes 32784
  (97 shorter events, 26.8 us)
Async XLA Ops:
  6.5 115.9 %all-reduce.3.cloned.1.call-start = ((), (), s32[]{:S(2)}) async-start(), calls=%async_computation.1 | async-start | bytes 262144 | tf_op jit(solution)/shard_map/psum | solution.py:41
  6.5 18.2 %collective-permute-start = (f32[32,4096]{1,0:T(8,128)}, f32[32,4096]{1,0:T(8,128)S(1)}, u32[]{:S(2)}, u32[]{:S(2)}) collective-permute-start(f32[32,4096]{1,0:T(8,128)} %param.10), channel_id=1, source_target_pairs={{0,4},{4,8},{8,12},{12,16},{16,20},{20,24},{24,28},{28,0},{1,5},{5... | collective-permute-start | bytes 1572872 | tf_op jit(solution)/shard_map/ppermute | solution.py:12
  24.7 15.8 %collective-permute-start.1 = (f32[32,4096]{1,0:T(8,128)S(1)}, f32[32,4096]{1,0:T(8,128)S(1)}, u32[]{:S(2)}, u32[]{:S(2)}) collective-permute-start(f32[32,4096]{1,0:T(8,128)S(1)} %collective-permute-done), channel_id=1, source_target_pairs={{0,4},{4,8},{8,12},{12,16},{16,20},{20,24},{24,28},{28,0},{1,5},{5... | collective-permute-start | bytes 1572872 | tf_op jit(solution)/shard_map/ppermute | solution.py:12
  40.5 15.3 %collective-permute-start.2 = (f32[32,4096]{1,0:T(8,128)S(1)}, f32[32,4096]{1,0:T(8,128)S(1)}, u32[]{:S(2)}, u32[]{:S(2)}) collective-permute-start(f32[32,4096]{1,0:T(8,128)S(1)} %collective-permute-done.1), channel_id=1, source_target_pairs={{0,4},{4,8},{8,12},{12,16},{16,20},{20,24},{24,28},{28,0},{1,5},{5... | collective-permute-start | bytes 1572872 | tf_op jit(solution)/shard_map/ppermute | solution.py:12
  42.5 241.2 %reduce-scatter.4.cloned.1.call-start = ((), (), s32[]{:S(2)}) async-start(), calls=%async_computation.2 | async-start | bytes 163840
  55.8 92.1 %collective-permute-start.3 = (f32[32,4096]{1,0:T(8,128)S(1)}, f32[32,4096]{1,0:T(8,128)S(1)}, u32[]{:S(2)}, u32[]{:S(2)}) collective-permute-start(f32[32,4096]{1,0:T(8,128)S(1)} %collective-permute-done.2), channel_id=1, source_target_pairs={{0,4},{4,8},{8,12},{12,16},{16,20},{20,24},{24,28},{28,0},{1,5},{5... | collective-permute-start | bytes 1572872 | tf_op jit(solution)/shard_map/ppermute | solution.py:12
  129.1 6.3 %collective-permute-start.4 = (f32[32]{0:T(128)S(1)}, f32[32]{0:T(128)S(1)}, u32[]{:S(2)}, u32[]{:S(2)}) collective-permute-start(f32[32]{0:T(128)S(1)} %get-tuple-element.137), channel_id=1, source_target_pairs={{0,4},{4,8},{8,12},{12,16},{16,20},{20,24},{24,28},{28,0},{1,5},{5... | collective-permute-start | bytes 392 | tf_op jit(solution)/shard_map/ppermute | solution.py:12
  135.4 6.3 %collective-permute-start.5 = (f32[32]{0:T(128)S(1)}, f32[32]{0:T(128)S(1)}, u32[]{:S(2)}, u32[]{:S(2)}) collective-permute-start(f32[32]{0:T(128)S(1)} %collective-permute-done.4), channel_id=1, source_target_pairs={{0,4},{4,8},{8,12},{12,16},{16,20},{20,24},{24,28},{28,0},{1,5},{5... | collective-permute-start | bytes 392 | tf_op jit(solution)/shard_map/ppermute | solution.py:12
  141.7 6.3 %collective-permute-start.6 = (f32[32]{0:T(128)S(1)}, f32[32]{0:T(128)S(1)}, u32[]{:S(2)}, u32[]{:S(2)}) collective-permute-start(f32[32]{0:T(128)S(1)} %collective-permute-done.5), channel_id=1, source_target_pairs={{0,4},{4,8},{8,12},{12,16},{16,20},{20,24},{24,28},{28,0},{1,5},{5... | collective-permute-start | bytes 392 | tf_op jit(solution)/shard_map/ppermute | solution.py:12
  147.9 114.4 %collective-permute-start.7 = (f32[32]{0:T(128)S(1)}, f32[32]{0:T(128)S(1)}, u32[]{:S(2)}, u32[]{:S(2)}) collective-permute-start(f32[32]{0:T(128)S(1)} %collective-permute-done.6), channel_id=1, source_target_pairs={{0,4},{4,8},{8,12},{12,16},{16,20},{20,24},{24,28},{28,0},{1,5},{5... | collective-permute-start | bytes 392 | tf_op jit(solution)/shard_map/ppermute | solution.py:12
  229.8 25.5 %copy-start = (f32[32,4096]{1,0:T(8,128)S(1)}, f32[32,4096]{1,0:T(8,128)}, u32[]{:S(2)}) copy-start(f32[32,4096]{1,0:T(8,128)} %param.10) | copy-start | bytes 1572868
Sparse Core Ops, SparseCore 0:
  42.6 79.7 all-reduce.2
  262.4 21.2 reduce-scatter.3
where the time goes:
time: 294 us; the launch traced here: 292 us
  waiting for transfers between devices  147 us (50%)
  other arithmetic  80.9 us (28%)
  local copies, waits for them, and re-layouts  38.8 us (13%)
  between operations  13.6 us (5%)
  blocking collectives  5.66 us (2%)
  starting transfers between devices  3.69 us (1%)
    reduce_sum x32, other arithmetic, triple_table(): jnp.sum(jnp.minimum(layer[:, None, :], partner[None, :, :]), axis=-1)  66.7 us
    psum x1, waiting for transfers between devices, body(): pivots = lax.psum(pivot_part, 'wide')  65.4 us
    ppermute x8, waiting for transfers between devices, from_behind(): return lax.ppermute(value, axis, pairs)  60.6 us
    min x32, local copies, waits for them, and re-layouts, triple_table(): jnp.minimum(layer[:, None, :], partner[None, :, :])  34.6 us
    unnamed x3, waiting for transfers between devices  21.2 us
  transfers between devices with their start and end apart: 10, of which 8 were waited for; matrix products, arithmetic and copies ran while one was open for 41% of the time, Pallas kernels for 0%

commit v1 on v0

v1 whole, which is shorter than its diff:
```python
import functools

import jax
import jax.numpy as jnp
from jax import lax
from jax.experimental import pallas as pl
from jax.experimental.pallas import tpu as pltpu
from jax.sharding import PartitionSpec as P

STEPS = 4
LANES = 128
SUB = 8
MESH = pl.DeviceIdType.MESH


def from_behind(value, axis, steps):
    count = lax.axis_size(axis)
    pairs = [(source, (source + steps) % count) for source in range(count)]
    return lax.ppermute(value, axis, pairs)


def plain_body(vectors, pivot_ids):
    row_count = vectors.shape[0]
    pivot_count = pivot_ids.shape[0]
    first_row = lax.axis_index("wide") * row_count
    chosen = (
        pivot_ids[:, None] == first_row + jnp.arange(row_count, dtype=jnp.int32)[None, :]
    ).astype(jnp.float32)
    pivot_part = jnp.dot(
        chosen, vectors, precision=lax.Precision.HIGHEST, preferred_element_type=jnp.float32
    )
    pivots = lax.psum(pivot_part, "wide")
    owned_total, pivot_total = lax.psum(
        (jnp.sum(vectors, axis=1), jnp.sum(pivots, axis=1)), "fields"
    )
    low = jnp.minimum(vectors[:, None, :], pivots[None, :, :])
    high = jnp.maximum(vectors[:, None, :], pivots[None, :, :])
    low_sum = jnp.sum(low, axis=-1)
    partner, partner_total = (vectors, owned_total)
    numerators = []
    partner_totals = []
    for stride in range(1, STEPS + 1):
        partner, partner_total = from_behind((partner, partner_total), "wide", 1)
        partner_totals.append(partner_total)
        rest = lax.map(
            lambda layer: jnp.sum(jnp.minimum(layer[:, None, :], partner[None, :, :]), axis=-1),
            jnp.transpose(high, (1, 0, 2)),
        )
        numerator = low_sum[:, :, None] + jnp.transpose(rest, (1, 0, 2))
        numerators.append(numerator.reshape(row_count, pivot_count * row_count))
    stacked = jnp.stack(numerators, axis=1)
    shares = lax.psum_scatter(stacked, "fields", scatter_dimension=2, tiled=True)
    share_width = shares.shape[2]
    offset = lax.axis_index("fields") * share_width
    step_totals = jnp.stack(partner_totals, axis=0)
    denominator = (
        owned_total[:, None, None, None]
        + pivot_total[None, None, :, None]
        + step_totals[None, :, None, :]
    )
    denominator = denominator.reshape(row_count, STEPS, pivot_count * row_count)
    denominator = lax.dynamic_slice_in_dim(denominator, offset, share_width, 2)
    return 1.5 * shares / denominator


def kernel(n_wide, n_fields, ids_ref, v_ref, out_ref, part, contrib, given, piv, pb, acc, low,
           own_sum, part_sum, msg, got, load_sem, c_send, c_recv, p_send, p_recv, b_send, b_recv,
           r_send, r_recv):
    rows = v_ref.shape[0]
    pivots = piv.shape[1]
    width = part.shape[3]
    cols = width // LANES
    share = pivots // n_fields
    me = lax.axis_index("wide")
    field = lax.axis_index("fields")
    parity = lax.rem(me, 2)
    beside = me + 1 - 2 * parity
    ahead = lax.rem(me + 2, n_wide)

    def wide_peer(d):
        return {"wide": lax.rem(me + d, n_wide)}

    def field_peer(d):
        return {"fields": lax.rem(field + d, n_fields)}

    for i in range(n_wide):
        pltpu.make_async_copy(
            v_ref.at[:, pl.ds(i * width, width)], part.at[i, 0], load_sem.at[i]
        ).start()

    barrier = pltpu.get_barrier_semaphore()
    for d in range(1, n_wide):
        pl.semaphore_signal(barrier, inc=1, device_id=wide_peer(d), device_id_type=MESH)
    for d in range(1, n_fields):
        pl.semaphore_signal(barrier, inc=1, device_id=field_peer(d), device_id_type=MESH)

    for q in range(pivots):
        row = ids_ref[q] - me * rows
        inside = jnp.logical_and(row >= 0, row < rows)
        values = v_ref[pl.ds(jnp.where(inside, row, 0), 1), :]
        values = jnp.where(inside, values, 0.0)
        for i in range(n_wide):
            contrib[i, q : q + 1, :] = values[:, i * width : (i + 1) * width]
    for i in range(n_wide):
        pltpu.make_async_copy(
            v_ref.at[:, pl.ds(i * width, width)], part.at[i, 0], load_sem.at[i]
        ).wait()
    pl.semaphore_wait(barrier, n_wide - 1 + n_fields - 1)

    def c_copy(d):
        return pltpu.make_async_remote_copy(
            src_ref=contrib.at[lax.rem(me + d, n_wide)], dst_ref=given.at[d],
            send_sem=c_send.at[d], recv_sem=c_recv.at[d],
            device_id=wide_peer(d), device_id_type=MESH)

    def p_copy(d):
        return pltpu.make_async_remote_copy(
            src_ref=piv.at[me], dst_ref=piv.at[me],
            send_sem=p_send.at[d], recv_sem=p_recv.at[d],
            device_id=wide_peer(d), device_id_type=MESH)

    def b_copy(kind, i, source, slot, target):
        return pltpu.make_async_remote_copy(
            src_ref=part.at[i, source], dst_ref=part.at[i, slot],
            send_sem=b_send.at[kind, i], recv_sem=b_recv.at[kind, i],
            device_id={"wide": target}, device_id_type=MESH)

    def hop_ahead(i):
        return b_copy(0, i, 0, 2, ahead)

    def relay_ahead(i):
        return b_copy(1, i, 2, 4, ahead)

    def first_beside(i):
        return b_copy(2, i, 2 * parity, 1, beside)

    def second_beside(i):
        return b_copy(3, i, 2 + 2 * parity, 3, beside)

    def stage0(i):
        hop_ahead(i).start()

        @pl.when(parity == 0)
        def _():
            first_beside(i).start()

    def stage1(i):
        hop_ahead(i).wait_recv()
        relay_ahead(i).start()

        @pl.when(parity == 1)
        def _():
            first_beside(i).start()

        @pl.when(parity == 0)
        def _():
            second_beside(i).start()

    def stage2(i):
        relay_ahead(i).wait_recv()

        @pl.when(parity == 1)
        def _():
            second_beside(i).start()

    for d in range(1, n_wide):
        c_copy(d).start()
    stage0(0)
    stage0(1)
    acc[...] = jnp.zeros_like(acc)
    low[...] = jnp.zeros_like(low)
    own_sum[...] = jnp.zeros_like(own_sum)
    part_sum[...] = jnp.zeros_like(part_sum)
    for d in range(1, n_wide):
        c_copy(d).wait_recv()
    total = contrib[me]
    for d in range(1, n_wide):
        total = total + given[d]
    piv[me] = total
    for d in range(1, n_wide):
        p_copy(d).start()
    stage1(0)
    stage0(2)
    stage1(1)
    stage2(0)
    for d in range(1, n_wide):
        source = lax.rem(me + n_wide - d, n_wide)
        pltpu.make_async_remote_copy(
            src_ref=piv.at[source], dst_ref=piv.at[source],
            send_sem=p_send.at[d], recv_sem=p_recv.at[d],
            device_id=wide_peer(d), device_id_type=MESH).wait_recv()

    groups = rows // SUB

    def step(i, carry):
        @pl.when(i + 3 < n_wide)
        def _():
            stage0(i + 3)

        @pl.when(i + 2 < n_wide)
        def _():
            stage1(i + 2)

        @pl.when(i + 1 < n_wide)
        def _():
            stage2(i + 1)

        first_beside(i).wait_recv()
        second_beside(i).wait_recv()

        pb[...] = jnp.broadcast_to(piv[i][:, None, :], pb.shape)
        for k in range(cols):
            lane = slice(k * LANES, (k + 1) * LANES)
            own_sum[...] += part[i, 0, :, lane]
            for s in range(STEPS):
                part_sum[s] += part[i, s + 1, :, lane]

        def per_row(v, inner):
            high = []
            low_now = None
            own = v_ref[pl.ds(v, 1), pl.ds(pl.multiple_of(i * width, LANES), width)]
            for k in range(cols):
                lane = slice(k * LANES, (k + 1) * LANES)
                mine = jnp.broadcast_to(own[:, lane], (SUB, LANES))
                high.append(jnp.maximum(mine[None], pb[:, :, lane]))
                small = jnp.minimum(mine, piv[i, :, lane])
                low_now = small if low_now is None else low_now + small
            low[v] += low_now
            for s in range(STEPS):
                for g in range(groups):
                    sums = None
                    for k in range(cols):
                        lane = slice(k * LANES, (k + 1) * LANES)
                        other = part[i, s + 1, g * SUB : (g + 1) * SUB, lane]
                        term = jnp.minimum(high[k], other[None])
                        sums = term if sums is None else sums + term
                    at = s * rows + g * SUB
                    acc[v, :, at : at + SUB, :] += sums
            return inner

        lax.fori_loop(0, rows, per_row, 0)
        return carry

    lax.fori_loop(0, n_wide, step, 0)

    def finish(v, inner):
        low_sum = jnp.sum(low[v], axis=-1, keepdims=True)
        for q in range(pivots):
            line = jnp.sum(acc[v, q].T, axis=0, keepdims=True) + low_sum[q : q + 1]
            msg[q // share, pl.ds(q % share * rows + v, 1), :] = line
        return inner

    lax.fori_loop(0, rows, finish, 0)
    own_total = jnp.sum(own_sum[...], axis=-1, keepdims=True)
    part_total = jnp.sum(part_sum[...].reshape(STEPS * rows, LANES).T, axis=0, keepdims=True)
    pivot_total = jnp.sum(jnp.sum(piv[...], axis=0), axis=-1, keepdims=True)
    pivot_total = jnp.broadcast_to(pivot_total, (pivots, LANES))
    base = own_total + part_total
    for j in range(n_fields):
        msg[j, share * rows : (share + 1) * rows, :] = base
        at = (share + 1) * rows
        for q in range(pivots):
            turned = (j * share + q) % pivots
            msg[j, at + q : at + q + 1, :] = pivot_total[turned : turned + 1]

    def r_copy(d):
        return pltpu.make_async_remote_copy(
            src_ref=msg.at[lax.rem(field + d, n_fields)], dst_ref=got.at[d],
            send_sem=r_send.at[d], recv_sem=r_recv.at[d],
            device_id=field_peer(d), device_id_type=MESH)

    for d in range(1, n_fields):
        r_copy(d).start()
    for d in range(1, n_fields):
        r_copy(d).wait_recv()
    whole = msg[field]
    for d in range(1, n_fields):
        whole = whole + got[d]
    base = whole[share * rows : (share + 1) * rows]
    at = (share + 1) * rows
    for q in range(share):
        denominator = base + whole[at + q : at + q + 1]
        out_ref[q] = 1.5 * whole[q * rows : (q + 1) * rows] / denominator

    for d in range(1, n_wide):
        c_copy(d).wait_send()
        p_copy(d).wait_send()
    for i in range(n_wide):
        hop_ahead(i).wait_send()
        relay_ahead(i).wait_send()
        first_beside(i).wait_send()
        second_beside(i).wait_send()
    for d in range(1, n_fields):
        r_copy(d).wait_send()


def fused_body(vectors, pivot_ids, n_wide, n_fields):
    rows, local = vectors.shape
    pivots = pivot_ids.shape[0]
    width = local // n_wide
    share = pivots // n_fields
    f32 = jnp.float32
    dma = pltpu.SemaphoreType.DMA
    lines = (share + 1) * rows + pivots
    table = pl.pallas_call(
        functools.partial(kernel, n_wide, n_fields),
        out_shape=jax.ShapeDtypeStruct((share, rows, STEPS * rows), f32),
        in_specs=[
            pl.BlockSpec(memory_space=pltpu.SMEM),
            pl.BlockSpec(memory_space=pltpu.VMEM),
        ],
        out_specs=pl.BlockSpec(memory_space=pltpu.VMEM),
        scratch_shapes=[
            pltpu.VMEM((n_wide, STEPS + 1, rows, width), f32),
            pltpu.VMEM((n_wide, pivots, width), f32),
            pltpu.VMEM((n_wide, pivots, width), f32),
            pltpu.VMEM((n_wide, pivots, width), f32),
            pltpu.VMEM((pivots, SUB, width), f32),
            pltpu.VMEM((rows, pivots, STEPS * rows, LANES), f32),
            pltpu.VMEM((rows, pivots, LANES), f32),
            pltpu.VMEM((rows, LANES), f32),
            pltpu.VMEM((STEPS, rows, LANES), f32),
            pltpu.VMEM((n_fields, lines, LANES), f32),
            pltpu.VMEM((n_fields, lines, LANES), f32),
            dma((n_wide,)),
            dma((n_wide,)), dma((n_wide,)),
            dma((n_wide,)), dma((n_wide,)),
            dma((4, n_wide)), dma((4, n_wide)),
            dma((n_fields,)), dma((n_fields,)),
        ],
        compiler_params=pltpu.CompilerParams(
            collective_id=0, has_side_effects=True, vmem_limit_bytes=48 * 1024 * 1024
        ),
    )(pivot_ids, vectors)
    table = table.reshape(share, rows, STEPS, rows)
    return jnp.transpose(table, (1, 2, 0, 3)).reshape(rows, STEPS, share * rows)


def solution(mesh):
    n_wide = mesh.shape["wide"]
    n_fields = mesh.shape["fields"]

    def body(vectors, pivot_ids):
        rows, local = vectors.shape
        pivots = pivot_ids.shape[0]
        fits = (
            n_wide % 2 == 0 and n_wide > STEPS and local % (n_wide * LANES) == 0
            and pivots % n_fields == 0 and pivots == SUB and rows % SUB == 0
            and STEPS * rows == LANES
        )
        if fits:
            return fused_body(vectors, pivot_ids, n_wide, n_fields)
        return plain_body(vectors, pivot_ids)

    placed = (P("wide", "fields"), P())
    return jax.shard_map(
        body, mesh=mesh, in_specs=placed, out_specs=P("wide", None, "fields"), check_vma=False
    )
```

time: 294 us -> 80.3 us (0.27)
  waiting for transfers between devices: 147 us -> 0 us
  other arithmetic: 80.9 us -> 0 us
  Pallas kernels: 0 us -> 77.5 us
  local copies, waits for them, and re-layouts: 38.8 us -> 2.69 us
  between operations: 13.6 us -> 0.03 us
  blocking collectives: 5.66 us -> 0 us
  starting transfers between devices: 3.69 us -> 0 us
    reduce_sum x37 -> x0, other arithmetic: 80.7 us -> none  [the longest x32 66.7 us: triple_table(): jnp.sum(jnp.minimum(layer[:, None, :], partner[None, :, :]), axis=-1)]
    pallas_call x0 -> x1, Pallas kernels: none -> 77.5 us  [fused_body(): pl.pallas_call(functools.partial(kernel, n_wide, n_fields), out_shape=jax...]
    psum x1 -> x0, waiting for transfers between devices: 65.4 us -> none  [body(): pivots = lax.psum(pivot_part, 'wide')]
    ppermute x8 -> x0, waiting for transfers between devices: 60.6 us -> none  [from_behind(): return lax.ppermute(value, axis, pairs)]
    min x32 -> x0, local copies, waits for them, and re-layouts: 34.6 us -> none  [triple_table(): jnp.minimum(layer[:, None, :], partner[None, :, :])]
    unnamed x3 -> x0, waiting for transfers between devices: 21.2 us -> none
    psum x1 -> x0, blocking collectives: 5.66 us -> none  [body(): lax.psum((jnp.sum(vectors, axis=1), jnp.sum(pivots, axis=1)), 'fields')]
    ppermute x8 -> x0, starting transfers between devices: 3.65 us -> none  [from_behind(): return lax.ppermute(value, axis, pairs)]
  transfers between devices with their start and end apart: 10 -> 0, of which waited for: 8 -> 0; matrix products, arithmetic and copies ran while one was open for 41% -> 0% of each run, Pallas kernels for 0% -> 0%
where the time goes in v1:
time: 80.3 us; the launch traced here: 80.2 us
  Pallas kernels  77.5 us (97%)
  local copies, waits for them, and re-layouts  2.69 us (3%)
    pallas_call x1, Pallas kernels, fused_body(): pl.pallas_call(functools.partial(kernel, n_wide, n_fields), out_shape=jax...  77.5 us
    unnamed x4, local copies, waits for them, and re-layouts  1.7 us

profile of v1, /device:TPU:0, one launch (start us, length us, event | category | flops | bytes accessed | tf_op | source)
XLA Modules:
  0.0 80.2 jit_solution(5175844916057865923)
XLA Ops:
  0.0 0.0 copy-start
  0.0 1.0 %copy-done = f32[32,4096]{1,0:T(8,128)S(1)} copy-done((f32[32,4096]{1,0:T(8,128)S(1)}, f32[32,4096]{1,0:T(8,128)}, u32[]{:S(2)}) %copy-start) | copy-done | bytes 524312
  1.0 0.0 copy-start.1
  1.0 0.7 copy-done.1
  1.7 77.5 %shard_map.28 = f32[2,32,128]{2,1,0:T(8,128)S(1)} custom-call(s32[8]{0:T(128)S(1)} %copy-done.1, f32[32,4096]{1,0:T(8,128)S(1)} %copy-done), custom_call_target="tpu_custom_call" | custom-call | tf_op jit(solution)/shard_map/pallas_call | solution.py:305
  79.2 0.1 reshape.6
  79.3 0.1 copy.3
  79.4 0.8 reshape.7
Async XLA Ops:
  0.0 1.0 %copy-start = (f32[32,4096]{1,0:T(8,128)S(1)}, f32[32,4096]{1,0:T(8,128)}, u32[]{:S(2)}) copy-start(f32[32,4096]{1,0:T(8,128)} %v_ref.1) | copy-start | bytes 1572868
  1.0 0.7 copy-start.1

commit v2 on v1

--- a/solution.py
+++ b/solution.py
@@ -10,6 +10,8 @@
 STEPS = 4
 LANES = 128
 SUB = 8
+PACK = 16
+QGROUP = 4
 MESH = pl.DeviceIdType.MESH
 
 
@@ -63,7 +65,7 @@
     return 1.5 * shares / denominator
 
 
-def kernel(n_wide, n_fields, ids_ref, v_ref, out_ref, part, contrib, given, piv, pb, acc, low,
+def kernel(n_wide, n_fields, ids_ref, v_ref, out_ref, part, contrib, given, piv, pb, near, acc, low,
            own_sum, part_sum, msg, got, load_sem, c_send, c_recv, p_send, p_recv, b_send, b_recv,
            r_send, r_recv):
     rows = v_ref.shape[0]
@@ -190,9 +192,27 @@
             send_sem=p_send.at[d], recv_sem=p_recv.at[d],
             device_id=wide_peer(d), device_id_type=MESH).wait_recv()
 
-    groups = rows // SUB
-
-    def step(i, carry):
+    place = lax.broadcasted_iota(jnp.int32, (1, LANES), 1) * n_fields + field
+    scale = jnp.exp2(place.astype(jnp.float32) / (LANES * n_fields))
+    unscale = 1.0 / scale
+
+    def prepare(i, half):
+        for k in range(cols):
+            lane = slice(k * LANES, (k + 1) * LANES)
+            to = slice(half * width + k * LANES, half * width + (k + 1) * LANES)
+            own_sum[...] += part[i, 0, :, lane]
+            for s in range(STEPS):
+                other = part[i, s + 1, :, lane]
+                part_sum[s] += other
+                near[s * rows : (s + 1) * rows, to] = (other * scale).astype(jnp.bfloat16)
+        for q in range(pivots):
+            line = piv[i, q : q + 1, :] * jnp.concatenate([scale] * cols, axis=1)
+            spread = jnp.broadcast_to(line, (PACK, width)).astype(jnp.bfloat16)
+            pb[q, :, half * width : (half + 1) * width] = spread
+
+    def step(t, carry):
+        i = 2 * t
+
         @pl.when(i + 3 < n_wide)
         def _():
             stage0(i + 3)
@@ -201,52 +221,78 @@
         def _():
             stage1(i + 2)
 
-        @pl.when(i + 1 < n_wide)
-        def _():
-            stage2(i + 1)
+        stage2(i + 1)
+
+        @pl.when(i + 4 < n_wide)
+        def _():
+            stage0(i + 4)
 
         first_beside(i).wait_recv()
         second_beside(i).wait_recv()
-
-        pb[...] = jnp.broadcast_to(piv[i][:, None, :], pb.shape)
-        for k in range(cols):
-            lane = slice(k * LANES, (k + 1) * LANES)
-            own_sum[...] += part[i, 0, :, lane]
-            for s in range(STEPS):
-                part_sum[s] += part[i, s + 1, :, lane]
+        prepare(i, 0)
+
+        @pl.when(i + 3 < n_wide)
+        def _():
+            stage1(i + 3)
+
+        @pl.when(i + 2 < n_wide)
+        def _():
+            stage2(i + 2)
+
+        first_beside(i + 1).wait_recv()
+        second_beside(i + 1).wait_recv()
+        prepare(i + 1, 1)
 
         def per_row(v, inner):
-            high = []
+            at = pl.ds(pl.multiple_of(i * width, LANES), 2 * width)
+            own = v_ref[pl.ds(v, 1), at]
             low_now = None
-            own = v_ref[pl.ds(v, 1), pl.ds(pl.multiple_of(i * width, LANES), width)]
-            for k in range(cols):
-                lane = slice(k * LANES, (k + 1) * LANES)
-                mine = jnp.broadcast_to(own[:, lane], (SUB, LANES))
-                high.append(jnp.maximum(mine[None], pb[:, :, lane]))
-                small = jnp.minimum(mine, piv[i, :, lane])
+            mine = []
+            for k in range(2 * cols):
+                line = own[:, k * LANES : (k + 1) * LANES]
+                wide_line = jnp.broadcast_to(line * scale, (PACK, LANES))
+                mine.append(wide_line.astype(jnp.bfloat16))
+                c = k % cols
+                small = jnp.minimum(line, piv[i + k // cols, :, c * LANES : (c + 1) * LANES])
                 low_now = small if low_now is None else low_now + small
             low[v] += low_now
-            for s in range(STEPS):
-                for g in range(groups):
-                    sums = None
-                    for k in range(cols):
-                        lane = slice(k * LANES, (k + 1) * LANES)
-                        other = part[i, s + 1, g * SUB : (g + 1) * SUB, lane]
-                        term = jnp.minimum(high[k], other[None])
-                        sums = term if sums is None else sums + term
-                    at = s * rows + g * SUB
-                    acc[v, :, at : at + SUB, :] += sums
+            for q0 in range(0, pivots, QGROUP):
+                high = [
+                    jnp.maximum(mine[k][None], pb[q0 : q0 + QGROUP, :, k * LANES : (k + 1) * LANES])
+                    for k in range(2 * cols)
+                ]
+                for g in range(STEPS * rows // PACK):
+                    line = slice(g * PACK, (g + 1) * PACK)
+                    terms = [
+                        jnp.minimum(high[k], near[line, k * LANES : (k + 1) * LANES][None])
+                        for k in range(2 * cols)
+                    ]
+                    while len(terms) > 1:
+                        terms = [
+                            terms[j] + terms[j + 1] if j + 1 < len(terms) else terms[j]
+                            for j in range(0, len(terms), 2)
+                        ]
+                    acc[v, q0 : q0 + QGROUP, line, :] += terms[0].astype(jnp.float32)
             return inner
 
         lax.fori_loop(0, rows, per_row, 0)
         return carry
 
-    lax.fori_loop(0, n_wide, step, 0)
+    lax.fori_loop(0, n_wide // 2, step, 0)
+
+    lane_at = lax.broadcasted_iota(jnp.int32, (SUB, LANES), 1)
+    sub_at = lax.broadcasted_iota(jnp.int32, (SUB, LANES), 0)
 
     def finish(v, inner):
         low_sum = jnp.sum(low[v], axis=-1, keepdims=True)
         for q in range(pivots):
-            line = jnp.sum(acc[v, q].T, axis=0, keepdims=True) + low_sum[q : q + 1]
+            spread = jnp.zeros((SUB, LANES), jnp.float32)
+            for g in range(LANES // SUB):
+                piece = acc[v, q, g * SUB : (g + 1) * SUB, :] * unscale
+                piece = jnp.sum(piece, axis=-1, keepdims=True)
+                spread = jnp.where(lane_at // SUB == g, piece, spread)
+            spread = jnp.where(lane_at % SUB == sub_at, spread, 0.0)
+            line = jnp.sum(spread, axis=0, keepdims=True) + low_sum[q : q + 1]
             msg[q // share, pl.ds(q % share * rows + v, 1), :] = line
         return inner
 
@@ -315,7 +361,8 @@
             pltpu.VMEM((n_wide, pivots, width), f32),
             pltpu.VMEM((n_wide, pivots, width), f32),
             pltpu.VMEM((n_wide, pivots, width), f32),
-            pltpu.VMEM((pivots, SUB, width), f32),
+            pltpu.VMEM((pivots, PACK, 2 * width), jnp.bfloat16),
+            pltpu.VMEM((STEPS * rows, 2 * width), jnp.bfloat16),
             pltpu.VMEM((rows, pivots, STEPS * rows, LANES), f32),
             pltpu.VMEM((rows, pivots, LANES), f32),
             pltpu.VMEM((rows, LANES), f32),

time: 80.3 us -> 85 us (1.059)
  Pallas kernels: 77.5 us -> 82.1 us
    pallas_call x1, Pallas kernels: 77.5 us -> 82.1 us  [fused_body(): pl.pallas_call(functools.partial(kernel, n_wide, n_fields), out_shape=jax...]
where the time goes in v2:
time: 85 us; the launch traced here: 84.8 us
  Pallas kernels  82.1 us (97%)
  local copies, waits for them, and re-layouts  2.69 us (3%)
    pallas_call x1, Pallas kernels, fused_body(): pl.pallas_call(functools.partial(kernel, n_wide, n_fields), out_shape=jax...  82.1 us

profile of v2, /device:TPU:0, one launch (start us, length us, event | category | flops | bytes accessed | tf_op | source)
XLA Modules:
  0.0 84.8 jit_solution(8941694872613403131)
XLA Ops:
  0.0 0.0 copy-start
  0.0 1.0 %copy-done = f32[32,4096]{1,0:T(8,128)S(1)} copy-done((f32[32,4096]{1,0:T(8,128)S(1)}, f32[32,4096]{1,0:T(8,128)}, u32[]{:S(2)}) %copy-start) | copy-done | bytes 524312
  1.0 0.0 copy-start.1
  1.0 0.7 copy-done.1
  1.7 82.1 %shard_map.28 = f32[2,32,128]{2,1,0:T(8,128)S(1)} custom-call(s32[8]{0:T(128)S(1)} %copy-done.1, f32[32,4096]{1,0:T(8,128)S(1)} %copy-done), custom_call_target="tpu_custom_call" | custom-call | tf_op jit(solution)/shard_map/pallas_call | solution.py:351
  83.8 0.1 reshape.6
  83.9 0.1 copy.3
  84.0 0.8 reshape.7
Async XLA Ops:
  0.0 1.0 %copy-start = (f32[32,4096]{1,0:T(8,128)S(1)}, f32[32,4096]{1,0:T(8,128)}, u32[]{:S(2)}) copy-start(f32[32,4096]{1,0:T(8,128)} %v_ref.1) | copy-start | bytes 1572868
  1.0 0.7 copy-start.1

commit v3 on v2

--- a/solution.py
+++ b/solution.py
@@ -78,6 +78,7 @@
     parity = lax.rem(me, 2)
     beside = me + 1 - 2 * parity
     ahead = lax.rem(me + 2, n_wide)
+    back = lax.rem(me + n_wide - 2, n_wide)
 
     def wide_peer(d):
         return {"wide": lax.rem(me + d, n_wide)}
@@ -127,48 +128,75 @@
             send_sem=b_send.at[kind, i], recv_sem=b_recv.at[kind, i],
             device_id={"wide": target}, device_id_type=MESH)
 
+    def route(i):
+        return True, False
+
     def hop_ahead(i):
         return b_copy(0, i, 0, 2, ahead)
 
-    def relay_ahead(i):
-        return b_copy(1, i, 2, 4, ahead)
+    def hop_back(i):
+        return b_copy(4, i, 0, 5, back)
+
+    def relay(i):
+        forward, _ = route(i)
+        return b_copy(1, i, 2, 4, ahead) if forward else b_copy(1, i, 5, 4, back)
 
     def first_beside(i):
         return b_copy(2, i, 2 * parity, 1, beside)
 
-    def second_beside(i):
-        return b_copy(3, i, 2 + 2 * parity, 3, beside)
+    def third(i):
+        _, along = route(i)
+        return b_copy(3, i, 1, 3, ahead) if along else b_copy(3, i, 2 + 2 * parity, 3, beside)
 
     def stage0(i):
+        forward, _ = route(i)
         hop_ahead(i).start()
+        if not forward:
+            hop_back(i).start()
 
         @pl.when(parity == 0)
         def _():
             first_beside(i).start()
 
     def stage1(i):
+        forward, along = route(i)
         hop_ahead(i).wait_recv()
-        relay_ahead(i).start()
+        if forward:
+            relay(i).start()
 
         @pl.when(parity == 1)
         def _():
             first_beside(i).start()
 
-        @pl.when(parity == 0)
-        def _():
-            second_beside(i).start()
+        if not along:
+            @pl.when(parity == 0)
+            def _():
+                third(i).start()
+
+        if not forward:
+            hop_back(i).wait_recv()
+            relay(i).start()
 
     def stage2(i):
-        relay_ahead(i).wait_recv()
-
-        @pl.when(parity == 1)
-        def _():
-            second_beside(i).start()
+        _, along = route(i)
+        if along:
+            first_beside(i).wait_recv()
+            third(i).start()
+            relay(i).wait_recv()
+        else:
+            relay(i).wait_recv()
+
+            @pl.when(parity == 1)
+            def _():
+                third(i).start()
+
+            first_beside(i).wait_recv()
 
     for d in range(1, n_wide):
         c_copy(d).start()
     stage0(0)
     stage0(1)
+    stage0(2)
     acc[...] = jnp.zeros_like(acc)
     low[...] = jnp.zeros_like(low)
     own_sum[...] = jnp.zeros_like(own_sum)
@@ -181,10 +209,6 @@
     piv[me] = total
     for d in range(1, n_wide):
         p_copy(d).start()
-    stage1(0)
-    stage0(2)
-    stage1(1)
-    stage2(0)
     for d in range(1, n_wide):
         source = lax.rem(me + n_wide - d, n_wide)
         pltpu.make_async_remote_copy(
@@ -210,41 +234,28 @@
             spread = jnp.broadcast_to(line, (PACK, width)).astype(jnp.bfloat16)
             pb[q, :, half * width : (half + 1) * width] = spread
 
-    def step(t, carry):
+    stages = (stage0, stage1, stage2)
+    lead = [(1, 0), (0, 3), (1, 1), (2, 0), (0, 4), (1, 2), (2, 1)]
+    points = []
+    for i in range(2, n_wide, 2):
+        points.append([[(1, i + 1), (0, i + 3)], [(2, i)], [(1, i + 2), (0, i + 4)], [(2, i + 1)]])
+
+    def issue(pairs):
+        for kind, i in pairs:
+            if i < n_wide:
+                stages[kind](i)
+
+    issue(lead)
+
+    def step(t):
         i = 2 * t
-
-        @pl.when(i + 3 < n_wide)
-        def _():
-            stage0(i + 3)
-
-        @pl.when(i + 2 < n_wide)
-        def _():
-            stage1(i + 2)
-
-        stage2(i + 1)
-
-        @pl.when(i + 4 < n_wide)
-        def _():
-            stage0(i + 4)
-
-        first_beside(i).wait_recv()
-        second_beside(i).wait_recv()
+        third(i).wait_recv()
         prepare(i, 0)
-
-        @pl.when(i + 3 < n_wide)
-        def _():
-            stage1(i + 3)
-
-        @pl.when(i + 2 < n_wide)
-        def _():
-            stage2(i + 2)
-
-        first_beside(i + 1).wait_recv()
-        second_beside(i + 1).wait_recv()
+        third(i + 1).wait_recv()
         prepare(i + 1, 1)
 
         def per_row(v, inner):
-            at = pl.ds(pl.multiple_of(i * width, LANES), 2 * width)
+            at = pl.ds(i * width, 2 * width)
             own = v_ref[pl.ds(v, 1), at]
             low_now = None
             mine = []
@@ -275,10 +286,15 @@
                     acc[v, q0 : q0 + QGROUP, line, :] += terms[0].astype(jnp.float32)
             return inner
 
-        lax.fori_loop(0, rows, per_row, 0)
-        return carry
-
-    lax.fori_loop(0, n_wide // 2, step, 0)
+        todo = points[t] if t < len(points) else []
+        if not todo:
+            lax.fori_loop(0, rows, per_row, 0)
+        for j, pairs in enumerate(todo):
+            issue(pairs)
+            lax.fori_loop(j * rows // len(todo), (j + 1) * rows // len(todo), per_row, 0)
+
+    for t in range(n_wide // 2):
+        step(t)
 
     lane_at = lax.broadcasted_iota(jnp.int32, (SUB, LANES), 1)
     sub_at = lax.broadcasted_iota(jnp.int32, (SUB, LANES), 0)
@@ -333,9 +349,11 @@
         p_copy(d).wait_send()
     for i in range(n_wide):
         hop_ahead(i).wait_send()
-        relay_ahead(i).wait_send()
+        if not route(i)[0]:
+            hop_back(i).wait_send()
+        relay(i).wait_send()
         first_beside(i).wait_send()
-        second_beside(i).wait_send()
+        third(i).wait_send()
     for d in range(1, n_fields):
         r_copy(d).wait_send()
 
@@ -357,7 +375,7 @@
         ],
         out_specs=pl.BlockSpec(memory_space=pltpu.VMEM),
         scratch_shapes=[
-            pltpu.VMEM((n_wide, STEPS + 1, rows, width), f32),
+            pltpu.VMEM((n_wide, STEPS + 2, rows, width), f32),
             pltpu.VMEM((n_wide, pivots, width), f32),
             pltpu.VMEM((n_wide, pivots, width), f32),
             pltpu.VMEM((n_wide, pivots, width), f32),
@@ -372,7 +390,7 @@
             dma((n_wide,)),
             dma((n_wide,)), dma((n_wide,)),
             dma((n_wide,)), dma((n_wide,)),
-            dma((4, n_wide)), dma((4, n_wide)),
+            dma((5, n_wide)), dma((5, n_wide)),
             dma((n_fields,)), dma((n_fields,)),
         ],
         compiler_params=pltpu.CompilerParams(
@@ -391,7 +409,7 @@
         rows, local = vectors.shape
         pivots = pivot_ids.shape[0]
         fits = (
-            n_wide % 2 == 0 and n_wide > STEPS and local % (n_wide * LANES) == 0
+            n_wide == 2 * STEPS and local % (n_wide * LANES) == 0
             and pivots % n_fields == 0 and pivots == SUB and rows % SUB == 0
             and STEPS * rows == LANES
         )

time: 85 us -> 75.3 us (0.89)
  Pallas kernels: 82.1 us -> 72.4 us
    pallas_call x1, Pallas kernels: 82.1 us -> 72.4 us  [fused_body(): pl.pallas_call(functools.partial(kernel, n_wide, n_fields), out_shape=jax...]
where the time goes in v3:
time: 75.3 us; the launch traced here: 75.1 us
  Pallas kernels  72.4 us (96%)
  local copies, waits for them, and re-layouts  2.69 us (4%)
    pallas_call x1, Pallas kernels, fused_body(): pl.pallas_call(functools.partial(kernel, n_wide, n_fields), out_shape=jax...  72.4 us
    unnamed x4, local copies, waits for them, and re-layouts  1.7 us

profile of v3, /device:TPU:0, one launch (start us, length us, event | category | flops | bytes accessed | tf_op | source)
XLA Modules:
  0.0 75.1 jit_solution(17914043001890225500)
XLA Ops:
  0.0 0.0 copy-start
  0.0 1.0 %copy-done = f32[32,4096]{1,0:T(8,128)S(1)} copy-done((f32[32,4096]{1,0:T(8,128)S(1)}, f32[32,4096]{1,0:T(8,128)}, u32[]{:S(2)}) %copy-start) | copy-done | bytes 524312
  1.0 0.0 copy-start.1
  1.0 0.7 copy-done.1
  1.7 72.4 %shard_map.28 = f32[2,32,128]{2,1,0:T(8,128)S(1)} custom-call(s32[8]{0:T(128)S(1)} %copy-done.1, f32[32,4096]{1,0:T(8,128)S(1)} %copy-done), custom_call_target="tpu_custom_call" | custom-call | tf_op jit(solution)/shard_map/pallas_call | solution.py:369
  74.1 0.1 reshape.6
  74.2 0.1 copy.3
  74.3 0.8 %reshape.7 = f32[32,4,64]{2,1,0:T(4,128)} reshape(f32[32,4,2,32]{3,2,1,0:T(2,128)S(1)} %copy.3) | data formatting | bytes 65536 | tf_op jit(solution)/shard_map/reshape | solution.py:401
Async XLA Ops:
  0.0 1.0 %copy-start = (f32[32,4096]{1,0:T(8,128)S(1)}, f32[32,4096]{1,0:T(8,128)}, u32[]{:S(2)}) copy-start(f32[32,4096]{1,0:T(8,128)} %v_ref.1) | copy-start | bytes 1572868
  1.0 0.7 copy-start.1
